TPU v7x, 512 devices: a whole 4x4x16 slice. The times are simulated.
512 devices in a mesh: node: 64 (over z_hi, y, x, core), local: 8 (over z_lo).
Axes of the slice: x: 4, y: 4, z: 16 (z_hi: 2, z_lo: 8; z = z_hi * 8 + z_lo), core: 2. Of those that a mesh axis runs over, the one named last changes fastest.
Arguments:
- tokens: bfloat16 [65536, 8192], P(('node', 'local')), may hold values from -24 to 24
- norm_gain: bfloat16 [8192], replicated, may hold values from 0.099609375 to 1.8984375
- key_weight: bfloat16 [8192, 128], P(('node', 'local')), may hold values from -0.0625 to 0.0625
- key_cotangent: bfloat16 [65536, 128], P(('node', 'local')), may hold values from -6 to 6
Outputs:
- keys: bfloat16 [65536, 128], P(('node', 'local'))
- token_grad: bfloat16 [65536, 8192], P(('node', 'local'))
- weight_grad: float32 [8192, 128], P(('node', 'local'))
- gain_grad: float32 [8192], replicated
All inputs are finite; a program needn't handle non-finite values.
Results may differ from a plain program's by a relative error of at most 0.005.
Values may be sent and summed in bfloat16 or wider, within the bound.
No kernel may reach another device: no remote copies, remote signals or barrier semaphores. Data moves between devices by JAX's collectives and lax.ppermute only.
A program may use at most 64 MiB of HBM per device.

v0:
```python
import math
import jax
import jax.numpy as jnp
from jax import lax
from jax.sharding import PartitionSpec as P


def local(tokens, norm_gain, key_weight, key_cotangent):
    nodes = lax.axis_size("node")
    locals_count = lax.axis_size("local")
    rows_dev = key_weight.shape[0]
    width = tokens.shape[1]
    tok_rows = tokens.shape[0]
    scale = 1.0 / math.sqrt(tok_rows * nodes * locals_count)
    gain_wide = norm_gain.astype(jnp.float32)
    wide = tokens.astype(jnp.float32)
    rstd = lax.rsqrt(jnp.mean(wide * wide, axis=1, keepdims=True) + 1e-05)
    normed = wide * rstd
    hidden = (normed * gain_wide).astype(jnp.bfloat16)
    secondary = lax.all_gather(key_weight, "node", axis=0, tiled=True)
    permuted = (
        hidden.reshape(tok_rows, nodes, locals_count, rows_dev)
        .transpose(0, 2, 1, 3)
        .reshape(tok_rows, width)
    )
    whole = lax.all_gather(secondary, "local", axis=0, tiled=True)
    keys_wide = jnp.dot(permuted, whole, preferred_element_type=jnp.float32)
    dpermuted = lax.dot_general(
        key_cotangent, whole, (((1,), (1,)), ((), ())), preferred_element_type=jnp.float32
    )
    keys = keys_wide.astype(jnp.bfloat16)
    dhidden = (
        dpermuted.reshape(tok_rows, locals_count, nodes, rows_dev)
        .transpose(0, 2, 1, 3)
        .reshape(tok_rows, width)
    )
    dnormed = dhidden * gain_wide
    inner = jnp.mean(dnormed * normed, axis=1, keepdims=True)
    token_grad = (rstd * (dnormed - normed * inner)).astype(jnp.bfloat16)
    gain_terms = jnp.sum(dhidden * normed, axis=0) * scale
    gain_grad = lax.psum(gain_terms, ("node", "local"))
    partial_grad = lax.psum_scatter(
        lax.dot_general(
            permuted, key_cotangent, (((0,), (0,)), ((), ())), preferred_element_type=jnp.float32
        )
        * scale,
        "local",
        scatter_dimension=0,
        tiled=True,
    )
    weight_grad = lax.psum_scatter(partial_grad, "node", scatter_dimension=0, tiled=True)
    return (keys, token_grad, weight_grad, gain_grad)


def solution(mesh):
    placed = (
        P(("node", "local"), None),
        P(),
        P(("node", "local"), None),
        P(("node", "local"), None),
    )
    return jax.shard_map(
        local,
        mesh=mesh,
        in_specs=placed,
        out_specs=(
            P(("node", "local"), None),
            P(("node", "local"), None),
            P(("node", "local"), None),
            P(),
        ),
        check_vma=False,
    )
```

profile of v0, /device:TPU:32, one launch (start us, length us, event | category | flops | bytes accessed | tf_op | source)
XLA Modules:
  0.0 929.3 jit_solution(14104093076151203116)
XLA Ops:
  7.2 0.0 copy-start
  7.2 0.0 copy-start.1
  7.2 0.0 all-gather.2.cloned.1.call-start
  7.2 169.5 %all_gather.6 = bf16[1024,128]{1,0:T(8,128)(2,1)} all-gather(bf16[16,128]{1,0:T(8,128)(2,1)} %param.6), channel_id=1, replica_groups=mesh['node'=64,'local'=8] {'node'}, dimensions={0}, use_global_device_ids=true | all-gather | bytes 266240 | tf_op jit(solution)/shard_map/all_gather | solution.py:20
  176.8 0.0 all-gather.2.cloned.1.call-update
  176.8 0.0 reduce-scatter.3.cloned.1.call-start
  176.8 3.2 copy.9
  180.1 0.0 copy-done.1
  180.1 1.1 fusion.10
  181.2 51.7 %all-gather.2.cloned.1.call-done = bf16[8192,128]{1,0:T(8,128)(2,1)} async-done(((bf16[1024,128]{1,0:T(8,128)(2,1)}), bf16[8192,128]{1,0:T(8,128)(2,1)}) %all-gather.2.cloned.1.call-update) | async-done | bytes 2097168 | tf_op jit(solution)/shard_map/all_gather | solution.py:26
  232.9 0.0 copy-done
  232.9 2.3 fusion.11
  235.2 0.6 copy.12
  235.8 2.6 fusion.9
  238.5 4.4 fusion.8
  242.9 0.4 copy.10
  243.3 2.6 convolution_multiply_fusion
  245.9 0.0 reduce-scatter.3.cloned.1.call-update
  245.9 0.0 reduce-scatter.5.cloned.1.call-start
  245.9 96.4 %reduce-scatter.3.cloned.1.call-done = f32[1024,128]{1,0:T(8,128)} async-done(((f32[8192,128]{1,0:T(8,128)}), f32[1024,128]{1,0:T(8,128)}) %reduce-scatter.3.cloned.1.call-update) | async-done | bytes 524304 | tf_op jit(solution)/shard_map/reduce_scatter | solution.py:42
  342.4 0.0 reduce-scatter.5.cloned.1.call-update
  342.4 4.1 copy.13
  346.5 111.4 %psum.7 = f32[8192]{0:T(1024)} all-reduce(f32[8192]{0:T(1024)S(1)} %broadcast_multiply_fusion), channel_id=1, replica_groups=mesh['node'=64,'local'=8] {'node','local'}, use_global_device_ids=true, to_apply=%region_5.0 | all-reduce | flops 8192 | bytes 65536 | tf_op jit(solution)/shard_map/psum | solution.py:41
  457.9 3.0 convolution_convert_fusion
  460.9 461.9 %reduce-scatter.5.cloned.1.call-done = f32[16,128]{1,0:T(8,128)} async-done(((f32[1024,128]{1,0:T(8,128)}), f32[16,128]{1,0:T(8,128)}) %reduce-scatter.5.cloned.1.call-update) | async-done | bytes 8208 | tf_op jit(solution)/shard_map/reduce_scatter | solution.py:51
  (4 shorter events, 0.0 us)
Async XLA Ops:
  7.2 225.7 %copy-start = (bf16[128,128]{1,0:T(8,128)(2,1)S(1)}, bf16[128,128]{1,0:T(8,128)(2,1)}, u32[]{:S(2)}) copy-start(bf16[128,128]{1,0:T(8,128)(2,1)} %param.7) | copy-start | bytes 98308
  7.2 172.9 %copy-start.1 = (bf16[8192]{0:T(1024)(128)(2,1)S(1)}, bf16[8192]{0:T(1024)(128)(2,1)}, u32[]{:S(2)}) copy-start(bf16[8192]{0:T(1024)(128)(2,1)} %param.5) | copy-start | bytes 49156
  7.2 225.7 %all-gather.2.cloned.1.call-start = ((), (), s32[]{:S(2)}) async-start(), calls=%async_computation.2 | async-start | bytes 2359296 | tf_op jit(solution)/shard_map/all_gather | solution.py:26
  176.8 165.6 %reduce-scatter.3.cloned.1.call-start = ((), (), s32[]{:S(2)}) async-start(), calls=%async_computation.3 | async-start | bytes 4718592 | tf_op jit(solution)/shard_map/reduce_scatter | solution.py:42
  245.9 676.9 %reduce-scatter.5.cloned.1.call-start = ((), (), s32[]{:S(2)}) async-start(), calls=%async_computation.4 | async-start | bytes 532480 | tf_op jit(solution)/shard_map/reduce_scatter | solution.py:51
Sparse Core Ops, SparseCore 0:
  176.9 55.9 all-gather.1
  246.0 96.3 reduce-scatter.2
  345.7 576.9 reduce-scatter.4
where the time goes:
time: 930 us; the launch traced here: 929 us
  waiting for transfers between devices  610 us (66%)
  blocking collectives  281 us (30%)
  between operations  13.8 us (1%)
    reduce_scatter x1, waiting for transfers between devices, local(): lax.psum_scatter(partial_grad, 'node', scatter_dimension=0, tiled=True)  462 us
    all_gather x1, blocking collectives, local(): secondary = lax.all_gather(key_weight, 'node', axis=0, tiled=True)  170 us
    psum x1, blocking collectives, local(): gain_grad = lax.psum(gain_terms, ('node', 'local'))  111 us
    reduce_scatter x1, waiting for transfers between devices, local(): lax.psum_scatter(lax.dot_general(permuted, key_cotangent, (((0,), (0,)),...  96.4 us
    all_gather x1, waiting for transfers between devices, local(): whole = lax.all_gather(secondary, 'local', axis=0, tiled=True)  51.7 us
  transfers between devices with their start and end apart: 3, of which 3 were waited for; matrix products, arithmetic and copies ran while one was open for 1% of the time, Pallas kernels for 0%

commit v1 on v0

--- a/solution.py
+++ b/solution.py
@@ -38,7 +38,7 @@
     inner = jnp.mean(dnormed * normed, axis=1, keepdims=True)
     token_grad = (rstd * (dnormed - normed * inner)).astype(jnp.bfloat16)
     gain_terms = jnp.sum(dhidden * normed, axis=0) * scale
-    gain_grad = lax.psum(gain_terms, ("node", "local"))
+    gain_grad = jnp.sum(lax.all_gather(gain_terms, ("node", "local")), axis=0)
     partial_grad = lax.psum_scatter(
         lax.dot_general(
             permuted, key_cotangent, (((0,), (0,)), ((), ())), preferred_element_type=jnp.float32

time: 930 us -> 2380 us (2.56)
  waiting for transfers between devices: 610 us -> 2140 us
  blocking collectives: 281 us -> 170 us
    all_gather x0 -> x1, waiting for transfers between devices: none -> 1440 us  [local(): gain_grad = jnp.sum(lax.all_gather(gain_terms, ('node', 'local')), axis=0)]
    psum x1 -> x0, blocking collectives: 111 us -> none  [local(): gain_grad = lax.psum(gain_terms, ('node', 'local'))]
    reduce_scatter x1, waiting for transfers between devices: 462 us -> 551 us  [local(): lax.psum_scatter(partial_grad, 'node', scatter_dimension=0, tiled=True)]
  transfers between devices with their start and end apart: 3 -> 4, of which waited for: 3 -> 4; matrix products, arithmetic and copies ran while one was open for 1% -> 2% of each run, Pallas kernels for 0% -> 0%
where the time goes in v1:
time: 2380 us
  waiting for transfers between devices  2140 us (90%)
  blocking collectives  170 us (7%)
  local copies, waits for them, and re-layouts  26.5 us (1%)
    all_gather x1, waiting for transfers between devices, local(): gain_grad = jnp.sum(lax.all_gather(gain_terms, ('node', 'local')), axis=0)  1440 us
    reduce_scatter x1, waiting for transfers between devices, local(): lax.psum_scatter(partial_grad, 'node', scatter_dimension=0, tiled=True)  551 us
    all_gather x1, blocking collectives, local(): secondary = lax.all_gather(key_weight, 'node', axis=0, tiled=True)  170 us
    reduce_scatter x1, waiting for transfers between devices, local(): lax.psum_scatter(lax.dot_general(permuted, key_cotangent, (((0,), (0,)),...  95.7 us
    all_gather x1, waiting for transfers between devices, local(): whole = lax.all_gather(secondary, 'local', axis=0, tiled=True)  51.7 us
  transfers between devices with their start and end apart: 4, of which 4 were waited for; matrix products, arithmetic and copies ran while one was open for 2% of the time, Pallas kernels for 0%

profile of v1, /device:TPU:32, one launch (start us, length us, event | category | flops | bytes accessed | tf_op | source)
XLA Modules:
  0.0 2376.0 jit_solution(14369778816381473888)
XLA Ops:
  7.2 0.0 copy-start
  7.2 0.0 copy-start.1
  7.2 0.0 all-gather.4.cloned.1.call-start
  7.2 169.5 %all_gather.10 = bf16[1024,128]{1,0:T(8,128)(2,1)} all-gather(bf16[16,128]{1,0:T(8,128)(2,1)} %param.6), channel_id=1, replica_groups=mesh['node'=64,'local'=8] {'node'}, dimensions={0}, use_global_device_ids=true | all-gather | bytes 266240 | tf_op jit(solution)/shard_map/all_gather | solution.py:20
  176.8 0.0 all-gather.4.cloned.1.call-update
  176.8 0.0 reduce-scatter.3.cloned.1.call-start
  176.8 3.2 copy.19
  180.1 0.0 copy-done.1
  180.1 1.1 fusion.10
  181.2 51.7 %all-gather.4.cloned.1.call-done = bf16[8192,128]{1,0:T(8,128)(2,1)} async-done(((bf16[1024,128]{1,0:T(8,128)(2,1)}), bf16[8192,128]{1,0:T(8,128)(2,1)}) %all-gather.4.cloned.1.call-update) | async-done | bytes 2097168 | tf_op jit(solution)/shard_map/all_gather | solution.py:26
  232.9 0.0 copy-done
  232.9 2.3 fusion.11
  235.2 0.6 copy.22
  235.8 2.6 fusion.9
  238.5 4.4 fusion.8
  242.9 0.4 copy.20
  243.2 2.6 convolution_multiply_fusion
  245.9 0.0 reduce-scatter.3.cloned.1.call-update
  245.9 0.0 all-gather.6.cloned.1.call-start
  245.9 0.6 broadcast_multiply_fusion
  246.6 0.1 all-gather.6.cloned.1.call-update
  246.6 0.0 reduce-scatter.5.cloned.1.call-start
  246.7 95.7 %reduce-scatter.3.cloned.1.call-done = f32[1024,128]{1,0:T(8,128)} async-done(((f32[8192,128]{1,0:T(8,128)}), f32[1024,128]{1,0:T(8,128)}) %reduce-scatter.3.cloned.1.call-update) | async-done | bytes 524304 | tf_op jit(solution)/shard_map/reduce_scatter | solution.py:42
  342.4 0.0 reduce-scatter.5.cloned.1.call-update
  342.4 4.1 copy.23
  346.5 3.0 convolution_convert_fusion
  349.4 1443.3 %all-gather.6.cloned.1.call-done = f32[4194304]{0:T(1024)} async-done(((f32[8192]{0:T(1024)}), f32[4194304]{0:T(1024)}) %all-gather.6.cloned.1.call-update) | async-done | bytes 16777232 | tf_op jit(solution)/shard_map/all_gather | solution.py:41
  1792.8 18.2 reshape.46
  1811.0 7.2 reduce_sum.39
  1818.2 551.3 %reduce-scatter.5.cloned.1.call-done = f32[16,128]{1,0:T(8,128)} async-done(((f32[1024,128]{1,0:T(8,128)}), f32[16,128]{1,0:T(8,128)}) %reduce-scatter.5.cloned.1.call-update) | async-done | bytes 8208 | tf_op jit(solution)/shard_map/reduce_scatter | solution.py:51
  (3 shorter events, 0.0 us)
Async XLA Ops:
  7.2 225.7 %copy-start = (bf16[128,128]{1,0:T(8,128)(2,1)S(1)}, bf16[128,128]{1,0:T(8,128)(2,1)}, u32[]{:S(2)}) copy-start(bf16[128,128]{1,0:T(8,128)(2,1)} %param.7) | copy-start | bytes 98308
  7.2 172.9 %copy-start.1 = (bf16[8192]{0:T(1024)(128)(2,1)S(1)}, bf16[8192]{0:T(1024)(128)(2,1)}, u32[]{:S(2)}) copy-start(bf16[8192]{0:T(1024)(128)(2,1)} %param.5) | copy-start | bytes 49156
  7.2 225.7 %all-gather.4.cloned.1.call-start = ((), (), s32[]{:S(2)}) async-start(), calls=%async_computation.2 | async-start | bytes 2359296 | tf_op jit(solution)/shard_map/all_gather | solution.py:26
  176.8 165.6 %reduce-scatter.3.cloned.1.call-start = ((), (), s32[]{:S(2)}) async-start(), calls=%async_computation.3 | async-start | bytes 4718592 | tf_op jit(solution)/shard_map/reduce_scatter | solution.py:42
  245.9 1546.9 %all-gather.6.cloned.1.call-start = ((), (), s32[]{:S(2)}) async-start(), calls=%async_computation.5 | async-start | bytes 16809984 | tf_op jit(solution)/shard_map/all_gather | solution.py:41
  246.6 2122.9 %reduce-scatter.5.cloned.1.call-start = ((), (), s32[]{:S(2)}) async-start(), calls=%async_computation.4 | async-start | bytes 532480 | tf_op jit(solution)/shard_map/reduce_scatter | solution.py:51
Sparse Core Ops, SparseCore 0:
  176.9 55.9 all-gather.3
  246.0 96.3 reduce-scatter.2
  345.2 1447.5 all-gather.5
  1796.0 573.4 reduce-scatter.4
